TPU v7x, 1024 devices: a whole 4x8x16 slice. The times are simulated.
1024 devices in a mesh: ctx: 256 (over z, y, x_lo), fsdp: 4 (over x_hi, core).
Axes of the slice: x: 4 (x_hi: 2, x_lo: 2; x = x_hi * 2 + x_lo), y: 8, z: 16, core: 2. Of those that a mesh axis runs over, the one named last changes fastest.
Arguments:
- features: bfloat16 [3, 32768, 6144], P(None, 'ctx', 'fsdp'), may hold values from -6 to 6
- cotangent: bfloat16 [32768, 6144], P('ctx', 'fsdp'), may hold values from -6 to 6
- master_filters: float32 [4, 7, 384], P(None, None, 'fsdp'), may hold values from -2 to 2
Outputs:
- mixed: bfloat16 [32768, 6144], P('ctx', 'fsdp')
- feature_grads: bfloat16 [3, 32768, 6144], P(None, 'ctx', 'fsdp')
- filter_grads: float32 [4, 7, 384], P(None, None, 'fsdp')
All inputs are finite; a program needn't handle non-finite values.
Results may differ from a plain program's by a relative error of at most 0.007.
Values may be sent and summed in bfloat16 or wider, within the bound.
A program may use at most 32 MiB of HBM per device.

v0:
```python
import math

import jax
import jax.numpy as jnp
from jax import lax
from jax.sharding import PartitionSpec as P


def from_behind(shard, axis, by):
    size = lax.axis_size(axis)
    pairs = [(i, i + by) for i in range(size) if 0 <= i + by < size]
    return lax.ppermute(shard, axis, pairs)


def causal(extended, weights):
    reach = weights.shape[0] - 1
    length = extended.shape[0] - reach
    result = weights[0] * extended[reach : reach + length]
    for lag in range(1, weights.shape[0]):
        result = result + weights[lag] * extended[reach - lag : reach - lag + length]
    return result


def anticausal(extended, weights):
    reach = weights.shape[0] - 1
    length = extended.shape[0] - reach
    result = weights[0] * extended[0:length]
    for lag in range(1, weights.shape[0]):
        result = result + weights[lag] * extended[lag : lag + length]
    return result


def per_device(features, cotangent, master_filters):
    gathered = lax.all_gather(
        master_filters.astype(jnp.bfloat16), "fsdp", axis=2, tiled=True
    ).astype(jnp.float32)
    groups = gathered.shape[2]
    repeats = features.shape[2] // groups
    weights = jnp.tile(gathered, (1, 1, repeats))
    reach = weights.shape[1] - 1
    length = features.shape[1]
    history = from_behind(features[:, length - reach :, :], "ctx", 1)
    inputs_ext = jnp.concatenate([history, features], axis=1).astype(jnp.float32)
    q_conv = causal(inputs_ext[0], weights[0])
    k_conv = causal(inputs_ext[1], weights[1])
    v_conv = causal(inputs_ext[2], weights[2])
    product = k_conv * v_conv
    prior = from_behind(product[length - reach :], "ctx", 1)
    product_ext = jnp.concatenate([prior, product], axis=0)
    mixer = causal(product_ext, weights[3])
    mixed = (q_conv * mixer).astype(jnp.bfloat16)
    upstream = cotangent.astype(jnp.float32)
    grad_qconv = upstream * mixer
    grad_mixer = upstream * q_conv
    head_product = anticausal(grad_mixer[: 2 * reach], weights[3])
    grad_khead = head_product * v_conv[:reach]
    grad_vhead = head_product * k_conv[:reach]
    incoming = from_behind(
        (grad_qconv[:reach], grad_khead, grad_vhead, grad_mixer[:reach]), "ctx", -1
    )
    grad_product = anticausal(jnp.concatenate([grad_mixer, incoming[3]], axis=0), weights[3])
    grad_kconv = grad_product * v_conv
    grad_vconv = grad_product * k_conv
    grad_q = anticausal(jnp.concatenate([grad_qconv, incoming[0]], axis=0), weights[0])
    grad_k = anticausal(jnp.concatenate([grad_kconv, incoming[1]], axis=0), weights[1])
    grad_v = anticausal(jnp.concatenate([grad_vconv, incoming[2]], axis=0), weights[2])
    feature_grads = jnp.stack([grad_q, grad_k, grad_v]).astype(jnp.bfloat16)
    pairs = (
        (grad_qconv, inputs_ext[0]),
        (grad_kconv, inputs_ext[1]),
        (grad_vconv, inputs_ext[2]),
        (grad_mixer, product_ext),
    )
    rows_out = []
    for grad_term, source in pairs:
        rows_out.append(
            jnp.stack(
                [
                    jnp.sum(grad_term * source[reach - lag : reach - lag + length], axis=0)
                    for lag in range(reach + 1)
                ]
            )
        )
    partial_sum = jnp.sum(jnp.stack(rows_out).reshape(4, reach + 1, repeats, groups), axis=2)
    count_all = length * lax.axis_size("ctx") * repeats * lax.axis_size("fsdp")
    factor = 1.0 / math.sqrt(count_all)
    summed = lax.psum(partial_sum, ("ctx", "fsdp"))
    portion = groups // lax.axis_size("fsdp")
    owned = lax.dynamic_slice_in_dim(summed, lax.axis_index("fsdp") * portion, portion, 2)
    filter_grads = owned * factor
    return (mixed, feature_grads, filter_grads)


def solution(mesh):
    return jax.shard_map(
        per_device,
        mesh=mesh,
        in_specs=(P(None, "ctx", "fsdp"), P("ctx", "fsdp"), P(None, None, "fsdp")),
        out_specs=(P("ctx", "fsdp"), P(None, "ctx", "fsdp"), P(None, None, "fsdp")),
        check_vma=False,
    )
```

profile of v0, /device:TPU:1, one launch (start us, length us, event | category | flops | bytes accessed | tf_op | source)
XLA Modules:
  0.0 263.9 jit_solution(6938237307471964428)
XLA Ops:
  0.6 0.9 slice.621
  1.5 3.9 %collective-permute-start = (bf16[3,6,1536]{2,1,0:T(8,128)(2,1)S(1)}, bf16[3,6,1536]{2,1,0:T(8,128)(2,1)S(1)}, u32[]{:S(2)}, u32[]{:S(2)}) collective-permute-start(bf16[3,6,1536]{2,1,0:T(8,128)(2,1)S(1)} %slice.621), channel_id=1, source_target_pairs={{0,4},{4,8},{8,12},{12,16},{16,20},{20,24},{24,28},{28,32},{32,36}... | collective-permute-start | bytes 165896 | tf_op jit(solution)/shard_map/ppermute | solution.py:12
  5.5 0.7 convert_element_type.16
  6.2 0.2 copy.10
  6.4 19.0 %all_gather.3 = bf16[4,7,384]{1,0,2:T(4,128)(2,1)S(1)} all-gather(bf16[4,7,96]{1,0,2:T(4,128)(2,1)S(1)} %copy.10), channel_id=1, replica_groups=mesh['ctx'=256,'fsdp'=4] {'fsdp'}, dimensions={2}, use_global_device_ids=true | all-gather | bytes 26880 | tf_op jit(solution)/shard_map/all_gather | solution.py:34
  25.3 0.1 convert_element_type.17
  25.4 12.8 %slice_reduce_fusion.19 = (f32[384]{0:T(512)S(1)}, f32[384]{0:T(512)S(1)}, f32[384]{0:T(512)S(1)}, f32[384]{0:T(512)S(1)}, f32[384]{0:T(512)S(1)}, /*index=5*/f3...) fusion(f32[4,7,384]{1,0,2:T(4,128)S(1)} %convert_element_type.17), kind=kLoop, calls=%fused_computation.198 | loop fusion | bytes 27648 | tf_op jit(solution)/shard_map/slice | solution.py:18
  38.5 0.0 copy-start.6
  38.5 0.0 collective-permute-done
  38.5 1.7 maximum_convert_fusion
  40.2 1.6 convert_multiply_fusion
  41.8 0.9 copy-done
  42.7 1.5 collective-permute-start.3
  44.1 28.8 %slice_reduce_fusion.20 = (f32[384]{0:T(512)S(1)}, f32[384]{0:T(512)S(1)}, f32[384]{0:T(512)S(1)}, f32[384]{0:T(512)S(1)}, f32[384]{0:T(512)S(1)}, /*index=5*/f3...) fusion(f32[4,7,384]{1,0,2:T(4,128)S(1)} %convert_element_type.17), kind=kLoop, calls=%fused_computation.199 | loop fusion | bytes 58368 | tf_op jit(solution)/shard_map/slice | solution.py:18
  73.4 0.7 tile.139
  74.1 0.7 tile.137
  74.8 0.0 collective-permute-done.3
  74.8 6.5 %multiply_reduce_fusion.14 = (f32[1536]{0:T(1024)}, f32[1536]{0:T(1024)S(1)}, f32[1536]{0:T(1024)S(1)}, f32[1536]{0:T(1024)S(1)}, f32[1536]{0:T(1024)S(1)}, /*in...) fusion(f32[3,134,1536]{2,1,0:T(8,128)S(1)} %maximum_convert_fusion,, ...), kind=kLoop, calls=%fused_computation.157 | loop fusion | flops 9229824 | bytes 14321664 | tf_op jit(solution)/shard_map/reduce_sum | solution.py:79
  81.3 1.3 stack.137
  82.6 0.6 stack.136
  83.2 0.6 stack.135
  83.8 0.6 stack.134
  84.4 0.6 stack.133
  85.0 0.6 stack.132
  85.6 1.5 slice_multiply_fusion.1
  87.1 1.4 collective-permute-start.4
  88.5 1.8 fusion.87
  90.3 4.6 %collective-permute-start.1 = (f32[6,1536]{1,0:T(8,128)S(1)}, f32[6,1536]{1,0:T(8,128)S(1)}, u32[]{:S(2)}, u32[]{:S(2)}) collective-permute-start(f32[6,1536]{1,0:T(8,128)S(1)} %slice.803), channel_id=1, source_target_pairs={{0,4},{4,8},{8,12},{12,16},{16,20},{20,24},{24,28},{28,32},{32,36}... | collective-permute-start | bytes 110600 | tf_op jit(solution)/shard_map/ppermute | solution.py:12
  95.1 0.6 slice_multiply_fusion
  95.7 1.5 collective-permute-start.5
  97.2 0.0 collective-permute-done.1
  97.2 1.4 multiply_reduce_fusion
  98.6 1.3 stack.153
  99.9 6.3 %multiply_reduce_fusion.21 = (f32[1536]{0:T(1024)}, f32[1536]{0:T(1024)}, f32[1536]{0:T(1024)}, f32[1536]{0:T(1024)}, f32[1536]{0:T(1024)}, /*index=5*/f32[1536]...) fusion(f32[3,134,1536]{2,1,0:T(8,128)S(1)} %maximum_convert_fus, ...), kind=kLoop, calls=%fused_computation.164 | loop fusion | flops 9808896 | bytes 16287744 | tf_op jit(solution)/shard_map/reduce_sum | solution.py:79
  106.2 0.7 stack.128
  106.9 0.7 stack.127
  107.6 0.7 stack.126
  108.3 0.7 stack.125
  109.0 0.7 stack.124
  109.7 0.7 stack.123
  110.4 0.7 stack.139
  111.2 0.7 stack.140
  111.9 0.8 stack.141
  112.7 0.7 stack.142
  113.4 0.7 stack.143
  114.1 0.7 stack.144
  114.8 0.7 stack.145
  115.5 0.7 stack.152
  116.2 0.7 stack.151
  116.9 0.7 stack.150
  117.6 0.7 stack.149
  118.3 0.7 stack.148
  119.0 0.7 stack.147
  119.7 0.6 slice.819
  120.3 1.3 collective-permute-start.2
  121.6 2.2 multiply_convert_fusion
  124.1 1.8 fusion.77
  125.9 0.1 maximum_reduce_fusion
  126.0 132.4 %psum.7 = f32[4,7,384]{2,1,0:T(8,128)S(1)} all-reduce(f32[4,7,384]{2,1,0:T(8,128)S(1)} %maximum_reduce_fusion), channel_id=1, replica_groups=mesh['ctx'=256,'fsdp'=4] {'ctx','fsdp'}, use_global_device_ids=true, to_apply=%region_29.0 | all-reduce | flops 10752 | bytes 86016 | tf_op jit(solution)/shard_map/psum | solution.py:87
  258.5 1.8 fusion.78
  260.2 0.1 dynamic-slice_multiply_fusion
  260.3 0.6 copy.11
  260.9 1.8 fusion.76
  262.7 1.1 pad_maximum_fusion
  (127 shorter events, 0.7 us)
Async XLA Ops:
  1.5 36.9 %collective-permute-start = (bf16[3,6,1536]{2,1,0:T(8,128)(2,1)S(1)}, bf16[3,6,1536]{2,1,0:T(8,128)(2,1)S(1)}, u32[]{:S(2)}, u32[]{:S(2)}) collective-permute-start(bf16[3,6,1536]{2,1,0:T(8,128)(2,1)S(1)} %slice.621), channel_id=1, source_target_pairs={{0,4},{4,8},{8,12},{12,16},{16,20},{20,24},{24,28},{28,32},{32,36}... | collective-permute-start | bytes 165896 | tf_op jit(solution)/shard_map/ppermute | solution.py:12
  38.4 1.8 copy-start.7
  38.4 1.7 copy-start.9
  38.5 1.7 copy-start.6
  41.8 0.9 copy-start
  42.7 32.1 %collective-permute-start.3 = (f32[6,1536]{1,0:T(8,128)S(1)}, f32[6,1536]{1,0:T(8,128)}, u32[]{:S(2)}, u32[]{:S(2)}) collective-permute-start(f32[6,1536]{1,0:T(8,128)S(1)} %slice.830), channel_id=1, source_target_pairs={{4,0},{8,4},{12,8},{16,12},{20,16},{24,20},{28,24},{32,28},{36,32}... | collective-permute-start | bytes 110600 | tf_op jit(solution)/shard_map/ppermute | solution.py:12
  74.8 10.8 %copy-start.1 = (f32[128,1536]{1,0:T(8,128)S(1)}, f32[128,1536]{1,0:T(8,128)}, u32[]{:S(2)}) copy-start(f32[128,1536]{1,0:T(8,128)} %copy-done) | copy-start | bytes 2359300
  87.1 7.9 %copy-start.20 = (f32[1,1,4,384]{3,2,1,0:T(4,128)S(1)}, f32[1,1,4,384]{3,2,1,0:T(4,128)}, u32[]{:S(2)}) copy-start(f32[1,1,4,384]{3,2,1,0:T(4,128)} %stack.132) | copy-start | bytes 18436
  87.1 7.9 %copy-start.19 = (f32[1,1,4,384]{3,2,1,0:T(4,128)S(1)}, f32[1,1,4,384]{3,2,1,0:T(4,128)}, u32[]{:S(2)}) copy-start(f32[1,1,4,384]{3,2,1,0:T(4,128)} %stack.133) | copy-start | bytes 18436
  87.1 8.0 %copy-start.18 = (f32[1,1,4,384]{3,2,1,0:T(4,128)S(1)}, f32[1,1,4,384]{3,2,1,0:T(4,128)}, u32[]{:S(2)}) copy-start(f32[1,1,4,384]{3,2,1,0:T(4,128)} %stack.134) | copy-start | bytes 18436
  87.1 8.0 %copy-start.17 = (f32[1,1,4,384]{3,2,1,0:T(4,128)S(1)}, f32[1,1,4,384]{3,2,1,0:T(4,128)}, u32[]{:S(2)}) copy-start(f32[1,1,4,384]{3,2,1,0:T(4,128)} %stack.135) | copy-start | bytes 18436
  87.1 8.0 %copy-start.16 = (f32[1,1,4,384]{3,2,1,0:T(4,128)S(1)}, f32[1,1,4,384]{3,2,1,0:T(4,128)}, u32[]{:S(2)}) copy-start(f32[1,1,4,384]{3,2,1,0:T(4,128)} %stack.136) | copy-start | bytes 18436
  87.1 37.0 %collective-permute-start.4 = (f32[6,1536]{1,0:T(8,128)}, f32[6,1536]{1,0:T(8,128)}, u32[]{:S(2)}, u32[]{:S(2)}) collective-permute-start(f32[6,1536]{1,0:T(8,128)} %get-tuple-element.78), channel_id=1, source_target_pairs={{4,0},{8,4},{12,8},{16,12},{20,16},{24,20},{28,24},{32,28},{36,32}... | collective-permute-start | bytes 110600 | tf_op jit(solution)/shard_map/ppermute | solution.py:12
  90.3 8.3 %copy-start.2 = (f32[128,1536]{1,0:T(8,128)}, f32[128,1536]{1,0:T(8,128)S(1)}, u32[]{:S(2)}) copy-start(f32[128,1536]{1,0:T(8,128)S(1)} %get-tuple-element.82) | copy-start | bytes 2359300
  90.3 8.3 %copy-start.3 = (f32[128,1536]{1,0:T(8,128)}, f32[128,1536]{1,0:T(8,128)S(1)}, u32[]{:S(2)}) copy-start(f32[128,1536]{1,0:T(8,128)S(1)} %get-tuple-element.83) | copy-start | bytes 2359300
  90.3 6.9 %collective-permute-start.1 = (f32[6,1536]{1,0:T(8,128)S(1)}, f32[6,1536]{1,0:T(8,128)S(1)}, u32[]{:S(2)}, u32[]{:S(2)}) collective-permute-start(f32[6,1536]{1,0:T(8,128)S(1)} %slice.803), channel_id=1, source_target_pairs={{0,4},{4,8},{8,12},{12,16},{16,20},{20,24},{24,28},{28,32},{32,36}... | collective-permute-start | bytes 110600 | tf_op jit(solution)/shard_map/ppermute | solution.py:12
  95.1 3.5 %copy-start.11 = (f32[1,7,4,384]{3,2,1,0:T(4,128)}, f32[1,7,4,384]{3,2,1,0:T(4,128)S(1)}, u32[]{:S(2)}) copy-start(f32[1,7,4,384]{3,2,1,0:T(4,128)S(1)} %constant_dynamic-update-slice_fusion.8) | copy-start | bytes 129028
  95.7 162.7 %collective-permute-start.5 = (f32[6,1536]{1,0:T(8,128)}, f32[6,1536]{1,0:T(8,128)}, u32[]{:S(2)}, u32[]{:S(2)}) collective-permute-start(f32[6,1536]{1,0:T(8,128)} %slice_multiply_fusion), channel_id=1, source_target_pairs={{4,0},{8,4},{12,8},{16,12},{20,16},{24,20},{28,24},{32,28},{36,32}... | collective-permute-start | bytes 110600 | tf_op jit(solution)/shard_map/ppermute | solution.py:12
  109.7 14.3 %copy-start.15 = (f32[1,1,4,384]{3,2,1,0:T(4,128)S(1)}, f32[1,1,4,384]{3,2,1,0:T(4,128)}, u32[]{:S(2)}) copy-start(f32[1,1,4,384]{3,2,1,0:T(4,128)} %stack.153) | copy-start | bytes 18436
  111.2 12.9 %copy-start.13 = (f32[1536]{0:T(1024)S(1)}, f32[1536]{0:T(1024)}, u32[]{:S(2)}) copy-start(f32[1536]{0:T(1024)} %get-tuple-element.9) | copy-start | bytes 18436
  111.9 12.2 %copy-start.5 = (f32[128,1536]{1,0:T(8,128)S(1)}, f32[128,1536]{1,0:T(8,128)}, u32[]{:S(2)}) copy-start(f32[128,1536]{1,0:T(8,128)} %get-tuple-element.72) | copy-start | bytes 2359300
  120.3 140.6 %collective-permute-start.2 = (f32[6,1536]{1,0:T(8,128)}, f32[6,1536]{1,0:T(8,128)}, u32[]{:S(2)}, u32[]{:S(2)}) collective-permute-start(f32[6,1536]{1,0:T(8,128)} %slice.819), channel_id=1, source_target_pairs={{4,0},{8,4},{12,8},{16,12},{20,16},{24,20},{28,24},{32,28},{36,32}... | collective-permute-start | bytes 110600 | tf_op jit(solution)/shard_map/ppermute | solution.py:12
  121.6 4.3 %copy-start.12 = (f32[1,7,4,384]{3,2,1,0:T(4,128)S(1)}, f32[1,7,4,384]{3,2,1,0:T(4,128)}, u32[]{:S(2)}) copy-start(f32[1,7,4,384]{3,2,1,0:T(4,128)} %copy-done.11) | copy-start | bytes 129028
  121.6 4.3 %copy-start.14 = (f32[1,1,4,384]{3,2,1,0:T(4,128)S(1)}, f32[1,1,4,384]{3,2,1,0:T(4,128)}, u32[]{:S(2)}) copy-start(f32[1,1,4,384]{3,2,1,0:T(4,128)} %stack.137) | copy-start | bytes 18436
  123.8 134.6 %copy-start.4 = (f32[128,1536]{1,0:T(8,128)S(1)}, f32[128,1536]{1,0:T(8,128)}, u32[]{:S(2)}) copy-start(f32[128,1536]{1,0:T(8,128)} %get-tuple-element.76) | copy-start | bytes 2359300
  124.1 136.9 %copy-start.8 = (f32[1536]{0:T(1024)S(1)}, f32[1536]{0:T(1024)}, u32[]{:S(2)}) copy-start(f32[1536]{0:T(1024)} %copy-done.7) | copy-start | bytes 18436
  124.1 136.9 %copy-start.10 = (f32[1536]{0:T(1024)S(1)}, f32[1536]{0:T(1024)}, u32[]{:S(2)}) copy-start(f32[1536]{0:T(1024)} %copy-done.9) | copy-start | bytes 18436
where the time goes:
time: 266 us; the launch traced here: 264 us
  blocking collectives  151 us (57%)
  local copies, waits for them, and re-layouts  66 us (25%)
  other arithmetic  31 us (12%)
  starting transfers between devices  14.2 us (5%)
    psum x1, blocking collectives, per_device(): summed = lax.psum(partial_sum, ('ctx', 'fsdp'))  132 us
    slice x2, local copies, waits for them, and re-layouts, causal(): result = weights[0] * extended[reach:reach + length]  41.7 us
    another operation x30, local copies, waits for them, and re-layouts, per_device(): jnp.stack([jnp.sum(grad_term * source[reach - lag:reach - lag + length],...  19.1 us
    all_gather x1, blocking collectives, per_device(): lax.all_gather(master_filters.astype(jnp.bfloat16), 'fsdp', axis=2, tiled...  19 us
    ppermute x6, starting transfers between devices, from_behind(): return lax.ppermute(shard, axis, pairs)  14.2 us
    reduce_sum x3, other arithmetic, per_device(): jnp.sum(grad_term * source[reach - lag:reach - lag + length], axis=0)  14.1 us
    another operation x4, other arithmetic, per_device(): feature_grads = jnp.stack([grad_q, grad_k, grad_v]).astype(jnp.bfloat16)  6.48 us
  transfers between devices with their start and end apart: 6, of which 0 were waited for; matrix products, arithmetic and copies ran while one was open for 29% of the time, Pallas kernels for 0%

commit v1 on v0

v1 whole, which is shorter than its diff:
```python
import functools
import math

import jax
import jax.numpy as jnp
from jax import lax
from jax.experimental import pallas as pl
from jax.experimental.pallas import tpu as pltpu
from jax.sharding import PartitionSpec as P

LO = 2
NY = 8
TAPS = 7
LANE = 128
F32 = jnp.float32
BF16 = jnp.bfloat16


def chunks(total, most=64):
    return [(at, min(most, total - at)) for at in range(0, total, most)]


def kernel(
    n_ctx, n_f, ny, factor,
    feat, cot, mast,
    mixed_o, grads_o, filt_o,
    hl_q, hl_kv, hr_c, hr_q, hr_kv, wg, wv,
    xq, xk, xv, xc, qc, kc, vc, pr, gm, gq, gk, gv, acc,
    s1s, s1r, s2s, s2r, s3s, s3r, res,
    halo_ss, halo_rs, filt_ss, filt_rs,
    s1_ss, s1_rs, s2_ss, s2_rs, s3_ss, s3_rs, s4_ss, s4_rs,
):
    length = feat.shape[1]
    blocks = feat.shape[2] // LANE
    portion = mast.shape[2]
    nz = n_ctx // (LO * ny)
    nx = n_f * LO
    ctx = lax.axis_index("ctx")
    f = lax.axis_index("fsdp")
    lo = lax.rem(ctx, LO)
    y = lax.rem(lax.div(ctx, LO), ny)
    z = lax.div(ctx, LO * ny)
    x8 = f * LO + lo

    def dev(z_, y_, lo_, f_):
        return ((z_ * ny + y_) * LO + lo_, f_)

    def row_dev(s):
        return dev(z, y, lax.rem(s, LO), lax.div(s, LO))

    nxt = (lax.rem(ctx + 1, n_ctx), f)
    prv = (lax.rem(ctx + n_ctx - 1, n_ctx), f)

    def remote(src, dst, ss, rs, device):
        return pltpu.make_async_remote_copy(
            src_ref=src, dst_ref=dst, send_sem=ss, recv_sem=rs,
            device_id=device, device_id_type=pl.DeviceIdType.MESH,
        )

    partners = [row_dev(lax.rem(x8 + d, nx)) for d in range(1, nx)]
    partners += [dev(z, lax.rem(y + d, ny), lo, f) for d in range(1, ny)]
    partners += [dev(lax.rem(z + d, nz), y, lo, f) for d in range(1, nz)]
    partners += [
        dev(z, lax.rem(y + d + ny, ny), 1 - lo, f) for d in (-2, -1, 1, 2)
    ]
    partners += [nxt, prv]
    barrier = pltpu.get_barrier_semaphore()
    for device in partners:
        pl.semaphore_signal(
            barrier, inc=1, device_id=device, device_id_type=pl.DeviceIdType.MESH
        )
    acc[...] = jnp.zeros_like(acc)
    wg[f] = mast[...]
    pl.semaphore_wait(barrier, len(partners))

    filt = []
    for d in range(1, n_f):
        copy = remote(
            mast, wg.at[f], filt_ss.at[d], filt_rs.at[f],
            (ctx, lax.rem(f + d, n_f)),
        )
        copy.start()
        filt.append(copy)
    halo_plan = [
        (feat.at[pl.ds(1, 2), pl.ds(length - 16, 16), :], hl_kv, nxt),
        (feat.at[0, pl.ds(length - 8, 8), :], hl_q, nxt),
        (cot.at[pl.ds(0, 16), :], hr_c, prv),
        (feat.at[0, pl.ds(0, 16), :], hr_q, prv),
        (feat.at[pl.ds(1, 2), pl.ds(0, 8), :], hr_kv, prv),
    ]
    halo = []
    for i, (src, dst, device) in enumerate(halo_plan):
        copy = remote(src, dst, halo_ss.at[i], halo_rs.at[i], device)
        copy.start()
        halo.append(copy)

    for d in range(1, n_f):
        src = lax.rem(f + d, n_f)
        remote(mast, wg.at[src], filt_ss.at[d], filt_rs.at[src], (ctx, src)).wait_recv()
    for j in range(TAPS):
        whole = jnp.concatenate([wg[i, j] for i in range(n_f)], axis=1)
        whole = whole.astype(BF16).astype(F32)
        for m in range(whole.shape[1] // LANE):
            wv[m, j] = whole[:, m * LANE : (m + 1) * LANE]
    for copy in halo:
        copy.wait_recv()

    tiles = wv.shape[0]
    first = ctx == 0
    last = ctx == n_ctx - 1

    def taps(m, bank):
        return [wv[m, j, pl.ds(bank, 1), :] for j in range(TAPS)]

    def fir(ref, at, rows, w, sign):
        total = w[0] * ref[pl.ds(at, rows), :]
        for j in range(1, TAPS):
            total = total + w[j] * ref[pl.ds(at + sign * j, rows), :]
        return total

    def first_pass(b, carry):
        m = lax.rem(b, tiles)
        lanes = pl.ds(pl.multiple_of(b * LANE, LANE), LANE)

        def edge(ref, drop):
            return jnp.where(drop, 0.0, ref[:, lanes].astype(F32))

        for ref, i in ((xq, 0), (xk, 1), (xv, 2)):
            ref[16 : 16 + length, :] = feat[i, :, lanes].astype(F32)
        xc[0:length, :] = cot[:, lanes].astype(F32)
        xq[8:16, :] = edge(hl_q, first)
        xk[0:16, :] = edge(hl_kv.at[0], first)
        xv[0:16, :] = edge(hl_kv.at[1], first)
        xc[length : length + 16, :] = edge(hr_c, last)
        xq[16 + length : 32 + length, :] = edge(hr_q, last)
        xk[16 + length : 24 + length, :] = edge(hr_kv.at[0], last)
        xv[16 + length : 24 + length, :] = edge(hr_kv.at[1], last)

        w = taps(m, 0)
        for at, rows in chunks(length + 16):
            conv = fir(xq, 16 + at, rows, w, -1)
            qc[at : at + rows, :] = conv
            gm[at : at + rows, :] = conv * xc[at : at + rows, :]
        w = taps(m, 1)
        for at, rows in chunks(length + 16):
            kc[at : at + rows, :] = fir(xk, 8 + at, rows, w, -1)
        w = taps(m, 2)
        for at, rows in chunks(length + 16):
            conv = fir(xv, 8 + at, rows, w, -1)
            vc[at : at + rows, :] = conv
            pr[at : at + rows, :] = conv * kc[at : at + rows, :]
        w = taps(m, 3)
        for at, rows in chunks(length + 8):
            mixer = fir(pr, 8 + at, rows, w, -1)
            gq[b, at : at + rows, :] = mixer * xc[at : at + rows, :]
            kept = min(rows, length - at)
            if kept > 0:
                mixed_o[at : at + kept, lanes] = (
                    mixer[:kept] * qc[at : at + kept, :]
                ).astype(BF16)
        for at, rows in chunks(length + 8):
            grad = fir(gm, at, rows, w, 1)
            gk[b, at : at + rows, :] = grad * vc[8 + at : 8 + at + rows, :]
            gv[b, at : at + rows, :] = grad * kc[8 + at : 8 + at + rows, :]

        for bank, (grad, source, off) in enumerate(
            ((gq.at[b], xq, 16), (gk.at[b], xk, 16), (gv.at[b], xv, 16), (gm, pr, 8))
        ):
            sums = [None] * TAPS
            for at, rows in chunks(length):
                g = grad[at : at + rows, :]
                for j in range(TAPS):
                    part = g * source[pl.ds(off + at - j, rows), :]
                    part = jnp.sum(part.reshape(rows // 8, 8, LANE), axis=0)
                    sums[j] = part if sums[j] is None else sums[j] + part
            for j in range(TAPS):
                acc[m, 4 * j + bank] = acc[m, 4 * j + bank] + sums[j]
        return carry

    lax.fori_loop(0, blocks, first_pass, 0)

    lane_at = lax.broadcasted_iota(jnp.int32, (8, LANE), 1)
    for pair in range(4):
        parts = [
            jnp.sum(acc[m, 8 * pair : 8 * pair + 8], axis=1) for m in range(tiles)
        ]
        for g in range(n_f):
            m, off = divmod(g * portion, LANE)
            piece = pltpu.roll(parts[m], (LANE - off) % LANE, 1) if off else parts[m]
            if off + portion > LANE:
                rest = pltpu.roll(parts[m + 1], LANE - off, 1)
                piece = jnp.where(lane_at < LANE - off, piece, rest)
            for i in range(2):
                half, tap = divmod(2 * pair + i, 4)
                s1s[g * LO + half, tap] = piece[4 * i : 4 * i + 4]
    sends = []
    for d in range(1, nx):
        s = lax.rem(x8 + d, nx)
        copy = remote(s1s.at[s], s1r.at[x8], s1_ss.at[d], s1_rs.at[x8], row_dev(s))
        copy.start()
        sends.append(copy)
    s1r[x8] = s1s[x8]
    for d in range(1, nx):
        s = lax.rem(x8 + d, nx)
        remote(s1s.at[s], s1r.at[s], s1_ss.at[d], s1_rs.at[s], row_dev(s)).wait_recv()
    total = s1r[0]
    for s in range(1, nx):
        total = total + s1r[s]
    s2s[...] = total

    mine = lax.rem(y, 4)
    for d in range(1, ny):
        s = lax.rem(y + d, ny)
        copy = remote(
            s2s.at[lax.rem(s, 4)], s2r.at[y], s2_ss.at[d], s2_rs.at[y], dev(z, s, lo, f)
        )
        copy.start()
        sends.append(copy)
    s2r[y] = s2s[mine]
    for d in range(1, ny):
        s = lax.rem(y + d, ny)
        remote(
            s2s.at[mine], s2r.at[s], s2_ss.at[d], s2_rs.at[s], dev(z, s, lo, f)
        ).wait_recv()
    total = s2r[0]
    for s in range(1, ny):
        total = total + s2r[s]
    s3s[...] = total

    for d in range(1, nz):
        s = lax.rem(z + d, nz)
        copy = remote(s3s, s3r.at[z], s3_ss.at[d], s3_rs.at[z], dev(s, y, lo, f))
        copy.start()
        sends.append(copy)
    s3r[z] = s3s[...]

    def second_pass(b, carry):
        m = lax.rem(b, tiles)
        lanes = pl.ds(pl.multiple_of(b * LANE, LANE), LANE)
        for bank, grad in enumerate((gq.at[b], gk.at[b], gv.at[b])):
            w = taps(m, bank)
            for at, rows in chunks(length):
                grads_o[bank, at : at + rows, lanes] = fir(grad, at, rows, w, 1).astype(BF16)
        return carry

    lax.fori_loop(0, blocks, second_pass, 0)

    for d in range(1, nz):
        s = lax.rem(z + d, nz)
        remote(s3s, s3r.at[s], s3_ss.at[d], s3_rs.at[s], dev(s, y, lo, f)).wait_recv()
    total = s3r[0]
    for s in range(1, nz):
        total = total + s3r[s]
    res[lo * 4 + mine] = total

    piece = res.at[lo * 4 + mine]
    n_send = 0
    for d in (0, -1, 1, 2):
        for other in (0, 1):
            if d == 0 and other == 0:
                continue
            lo_ = 1 - lo if other else lo
            copy = remote(
                piece, piece, s4_ss.at[n_send], s4_rs.at[lo * 4 + mine],
                dev(z, lax.rem(y + d + ny, ny), lo_, f),
            )
            copy.start()
            sends.append(copy)
            n_send += 1
    for d in range(1, LO * 4):
        s = lax.rem(lo * 4 + mine + d, LO * 4)
        remote(piece, res.at[s], s4_ss.at[0], s4_rs.at[s], nxt).wait_recv()
    for j in range(TAPS):
        filt_o[j] = res[j][:, :portion] * factor

    for copy in filt + halo + sends:
        copy.wait_send()


def per_device(n_ctx, n_f, ny, features, cotangent, master_filters):
    _, length, width = features.shape
    portion = master_filters.shape[2]
    groups = portion * n_f
    repeats = width // groups
    count_all = length * n_ctx * repeats * n_f
    factor = 1.0 / math.sqrt(count_all)
    nz = n_ctx // (LO * ny)
    nx = n_f * LO
    blocks = width // LANE
    tiles = groups // LANE
    vm = pltpu.VMEM
    dma = pltpu.SemaphoreType.DMA
    scratch = [
        vm((8, width), BF16), vm((2, 16, width), BF16),
        vm((16, width), BF16), vm((16, width), BF16), vm((2, 8, width), BF16),
        vm((n_f, TAPS, 4, portion), F32), vm((tiles, TAPS, 4, LANE), F32),
    ]
    scratch += [vm((length + 32, LANE), F32)] * 3 + [vm((length + 16, LANE), F32)] * 6
    scratch += [vm((blocks, length + 8, LANE), F32)] * 3
    scratch += [
        vm((tiles, 32, 8, LANE), F32),
        vm((nx, 4, 4, LANE), F32), vm((nx, 4, 4, LANE), F32),
        vm((4, 4, LANE), F32), vm((ny, 4, LANE), F32),
        vm((4, LANE), F32), vm((nz, 4, LANE), F32), vm((8, 4, LANE), F32),
        dma((5,)), dma((5,)), dma((n_f,)), dma((n_f,)),
        dma((nx,)), dma((nx,)), dma((ny,)), dma((ny,)), dma((nz,)), dma((nz,)),
        dma((7,)), dma((8,)),
    ]
    vmem = pl.BlockSpec(memory_space=pltpu.MemorySpace.VMEM)
    mixed, grads, filters = pl.pallas_call(
        functools.partial(kernel, n_ctx, n_f, ny, factor),
        out_shape=(
            jax.ShapeDtypeStruct((length, width), BF16),
            jax.ShapeDtypeStruct((3, length, width), BF16),
            jax.ShapeDtypeStruct((TAPS, 4, portion), F32),
        ),
        in_specs=[vmem] * 3,
        out_specs=(vmem, vmem, vmem),
        scratch_shapes=scratch,
        compiler_params=pltpu.CompilerParams(
            collective_id=0, has_side_effects=True, vmem_limit_bytes=40 * 1024 * 1024
        ),
    )(features, cotangent, jnp.transpose(master_filters, (1, 0, 2)))
    return mixed, grads, jnp.transpose(filters, (1, 0, 2))


def solution(mesh, ny=NY):
    return jax.shard_map(
        functools.partial(per_device, mesh.shape["ctx"], mesh.shape["fsdp"], ny),
        mesh=mesh,
        in_specs=(P(None, "ctx", "fsdp"), P("ctx", "fsdp"), P(None, None, "fsdp")),
        out_specs=(P("ctx", "fsdp"), P(None, "ctx", "fsdp"), P(None, None, "fsdp")),
        check_vma=False,
    )
```

time: 266 us -> 61.2 us (0.23)
  the two profiles are of different devices: /device:TPU:1 before, /device:TPU:2 now
where the time goes in v1:
time: 61.2 us; the launch traced here: 61 us
  Pallas kernels  55 us (90%)
  local copies, waits for them, and re-layouts  5.33 us (9%)
  between operations  0.65 us (1%)
    pallas_call x1, Pallas kernels, per_device(): pl.pallas_call(functools.partial(kernel, n_ctx, n_f, ny, factor), out_sha...  55 us
    unnamed x9, local copies, waits for them, and re-layouts  5.33 us

profile of v1, /device:TPU:2, one launch (start us, length us, event | category | flops | bytes accessed | tf_op | source)
XLA Modules:
  0.0 61.0 jit_solution(14936070714399161114)
XLA Ops:
  0.6 0.0 copy-start
  0.6 1.3 %copy-done = bf16[3,128,1536]{2,1,0:T(8,128)(2,1)S(1)} copy-done((bf16[3,128,1536]{2,1,0:T(8,128)(2,1)S(1)}, bf16[3,128,1536]{2,1,0:T(8,128)(2,1)}, u32[]{:S(2)}) %copy-start) | copy-done | bytes 1179672
  1.9 0.0 copy-start.1
  1.9 1.0 %copy-done.1 = bf16[128,1536]{1,0:T(8,128)(2,1)S(1)} copy-done((bf16[128,1536]{1,0:T(8,128)(2,1)S(1)}, bf16[128,1536]{1,0:T(8,128)(2,1)}, u32[]{:S(2)}) %copy-start.1) | copy-done | bytes 393240
  2.9 0.0 copy-start.2
  2.9 0.7 %copy-done.2 = f32[4,7,96]{2,0,1:T(4,128)S(1)} copy-done((f32[4,7,96]{2,0,1:T(4,128)S(1)}, f32[4,7,96]{2,0,1:T(4,128)}, u32[]{:S(2)}) %copy-start.2) | copy-done | bytes 10776
  3.6 55.0 %shard_map.58 = (bf16[128,1536]{1,0:T(8,128)(2,1)S(1)}, bf16[3,128,1536]{2,1,0:T(8,128)(2,1)S(1)}, f32[7,4,96]{2,1,0:T(4,128)S(1)}) custom-call(bf16[3,128,1536]{2,1,0:T(8,128)(2,1)S(1)} %copy-done, bf16[128,1536]{1,0:T(8,128)(2,1)S(1)} %copy-done.1, f32[7,4,96]{2,1,0:T(4,128)S(1)} %bitcast.2), custom_call_target="tpu_custom_call" | custom-call | tf_op jit(solution)/shard_map/pallas_call | solution.py:310
  58.6 0.7 %copy.9 = bf16[128,1536]{1,0:T(8,128)(2,1)} copy(bf16[128,1536]{1,0:T(8,128)(2,1)S(1)} %get-tuple-element.12) | data formatting | bytes 786432
  59.4 1.0 %copy.10 = bf16[3,128,1536]{2,1,0:T(8,128)(2,1)} copy(bf16[3,128,1536]{2,1,0:T(8,128)(2,1)S(1)} %get-tuple-element.13) | data formatting | bytes 2359296
  60.4 0.6 copy.11
Async XLA Ops:
  0.6 1.3 %copy-start = (bf16[3,128,1536]{2,1,0:T(8,128)(2,1)S(1)}, bf16[3,128,1536]{2,1,0:T(8,128)(2,1)}, u32[]{:S(2)}) copy-start(bf16[3,128,1536]{2,1,0:T(8,128)(2,1)} %feat.1) | copy-start | bytes 3538948
  1.9 1.0 %copy-start.1 = (bf16[128,1536]{1,0:T(8,128)(2,1)S(1)}, bf16[128,1536]{1,0:T(8,128)(2,1)}, u32[]{:S(2)}) copy-start(bf16[128,1536]{1,0:T(8,128)(2,1)} %cot.1) | copy-start | bytes 1179652
  2.9 0.7 %copy-start.2 = (f32[4,7,96]{2,0,1:T(4,128)S(1)}, f32[4,7,96]{2,0,1:T(4,128)}, u32[]{:S(2)}) copy-start(f32[4,7,96]{2,0,1:T(4,128)} %param.5) | copy-start | bytes 32260

commit v2 on v1

v2 whole, which is shorter than its diff:
```python
import functools
import math

import jax
import jax.numpy as jnp
from jax import lax
from jax.experimental import pallas as pl
from jax.experimental.pallas import tpu as pltpu
from jax.sharding import PartitionSpec as P

LO = 2
NY = 8
TAPS = 7
LANE = 128
F32 = jnp.float32
BF16 = jnp.bfloat16
ALL_VMEM = 67043328


def chunks(first, end, most=64):
    return [(at, min(most, end - at)) for at in range(first, end, most)]


def far_first(n):
    return sorted(range(1, n), key=lambda d: -min(d, n - d))


def kernel(
    n_ctx, n_f, ny,
    feat, cot, mast,
    mixed_o, grads_o, res,
    fb, cb, mb, gb, hl_q, hl_kv, hr_c, hr_q, lr_c, lr_q, lr_kv, wg, wv,
    xq, xk, xv, xc, qc, kc, vc, pr, gm, gq, gk, gv, acc,
    s1s, s1r, s2s, s2r, s3s, s3r, s4s,
    load_sem, halo_ss, halo_rs, filt_ss, filt_rs,
    s1_ss, s1_rs, s2_ss, s2_rs, s3_ss, s3_rs, s4_ss, s4_rs, out_sem, near_sem,
):
    length = fb.shape[1]
    blocks = fb.shape[2] // LANE
    portion = mast.shape[2]
    tiles = wv.shape[0]
    nz = n_ctx // (LO * ny)
    nx = n_f * LO
    ctx = lax.axis_index("ctx")
    f = lax.axis_index("fsdp")
    lo = lax.rem(ctx, LO)
    y = lax.rem(lax.div(ctx, LO), ny)
    z = lax.div(ctx, LO * ny)
    x8 = f * LO + lo
    first = ctx == 0
    last = ctx == n_ctx - 1

    def dev(z_, y_, lo_, f_):
        return ((z_ * ny + y_) * LO + lo_, f_)

    def row_dev(s):
        return dev(z, y, lax.rem(s, LO), lax.div(s, LO))

    nxt = (lax.rem(ctx + 1, n_ctx), f)
    prv = (lax.rem(ctx + n_ctx - 1, n_ctx), f)

    def remote(src, dst, ss, rs, device):
        return pltpu.make_async_remote_copy(
            src_ref=src, dst_ref=dst, send_sem=ss, recv_sem=rs,
            device_id=device, device_id_type=pl.DeviceIdType.MESH,
        )

    def at_z(d):
        return dev(lax.rem(z + d + nz, nz), y, lo, f)

    def at_y(d):
        return dev(z, lax.rem(y + d + ny, ny), lo, f)

    partners = [nxt, prv]
    if nz > 1:
        partners += [at_z(1), at_z(-1)]
    if ny > 1:
        partners += [at_y(1), at_y(-1)]
    partners += [row_dev(lax.rem(x8 + d, nx)) for d in range(1, nx)]
    barrier = pltpu.get_barrier_semaphore()
    for device in partners:
        pl.semaphore_signal(
            barrier, inc=1, device_id=device, device_id_type=pl.DeviceIdType.MESH
        )
    loads = [
        pltpu.make_async_copy(feat, fb, load_sem.at[0]),
        pltpu.make_async_copy(cot, cb, load_sem.at[1]),
        pltpu.make_async_copy(mast, wg.at[f], load_sem.at[2]),
    ]
    for copy in loads:
        copy.start()
    acc[...] = jnp.zeros_like(acc)
    pl.semaphore_wait(barrier, len(partners))

    def tell(step):
        reach = 1 << step
        for i, (n, at) in enumerate(((nz, at_z), (ny, at_y))):
            if reach < n // 2:
                for d in (reach, -reach):
                    pl.semaphore_signal(
                        near_sem.at[step, i], inc=1, device_id=at(d),
                        device_id_type=pl.DeviceIdType.MESH,
                    )

    def hear(step):
        reach = 1 << step
        for i, n in enumerate((nz, ny)):
            if reach < n // 2:
                pl.semaphore_wait(near_sem.at[step, i], 2)

    tell(0)

    kept = []
    for d in range(1, n_f):
        copy = remote(
            mast, wg.at[f], filt_ss.at[d], filt_rs.at[f],
            (ctx, lax.rem(f + d, n_f)),
        )
        copy.start()
        kept.append(copy)
    halo_plan = [
        (feat.at[pl.ds(1, 2), pl.ds(length - 16, 16), :], hl_kv, nxt),
        (feat.at[0, pl.ds(length - 8, 8), :], hl_q, nxt),
        (cot.at[pl.ds(0, 8), :], hr_c, prv),
        (feat.at[0, pl.ds(0, 8), :], hr_q, prv),
        (cot.at[pl.ds(8, 8), :], lr_c, prv),
        (feat.at[0, pl.ds(8, 8), :], lr_q, prv),
        (feat.at[pl.ds(1, 2), pl.ds(0, 8), :], lr_kv, prv),
    ]
    halo = []
    for i, (src, dst, device) in enumerate(halo_plan):
        copy = remote(src, dst, halo_ss.at[i], halo_rs.at[i], device)
        if i < 4:
            copy.start()
        halo.append(copy)
    kept += halo

    for copy in loads:
        copy.wait()
    for d in range(1, n_f):
        src = lax.rem(f + d, n_f)
        remote(mast, wg.at[src], filt_ss.at[d], filt_rs.at[src], (ctx, src)).wait_recv()
    hear(0)
    tell(1)
    for j in range(TAPS):
        whole = jnp.concatenate([wg[i, j] for i in range(n_f)], axis=1)
        whole = whole.astype(BF16).astype(F32)
        for m in range(tiles):
            wv[m, j] = whole[:, m * LANE : (m + 1) * LANE]

    def taps(m, bank):
        return [wv[m, j, pl.ds(bank, 1), :] for j in range(TAPS)]

    def fir(ref, at, rows, w, sign):
        total = w[0] * ref[pl.ds(at, rows), :]
        for j in range(1, TAPS):
            total = total + w[j] * ref[pl.ds(at + sign * j, rows), :]
        return total

    def lanes_of(b):
        return pl.ds(pl.multiple_of(b * LANE, LANE), LANE)

    def q_rows(b, m, spans):
        w = taps(m, 0)
        for at, rows in spans:
            conv = fir(xq.at[b], 16 + at, rows, w, -1)
            qc[b, at : at + rows, :] = conv
            gm[b, at : at + rows, :] = conv * xc[b, at : at + rows, :]

    def kv_rows(b, m, spans):
        w = taps(m, 1)
        for at, rows in spans:
            kc[b, 8 + at : 8 + at + rows, :] = fir(xk.at[b], 16 + at, rows, w, -1)
        w = taps(m, 2)
        for at, rows in spans:
            own = slice(8 + at, 8 + at + rows)
            conv = fir(xv.at[b], 16 + at, rows, w, -1)
            vc[b, own, :] = conv
            pr[b, own, :] = conv * kc[b, own, :]

    def mixer_rows(b, m, spans, keep=True):
        w = taps(m, 3)
        for at, rows in spans:
            mixer = fir(pr.at[b], 8 + at, rows, w, -1)
            gq[b, at : at + rows, :] = mixer * xc[b, at : at + rows, :]
            if keep:
                mb[at : at + rows, lanes_of(b)] = (
                    mixer * qc[b, at : at + rows, :]
                ).astype(BF16)

    def product_rows(b, m, spans):
        w = taps(m, 3)
        for at, rows in spans:
            own = slice(8 + at, 8 + at + rows)
            grad = fir(gm.at[b], at, rows, w, 1)
            gk[b, at : at + rows, :] = grad * vc[b, own, :]
            gv[b, at : at + rows, :] = grad * kc[b, own, :]

    def filter_rows(b, m, bank, spans):
        grad = (gq, gk, gv, gm)[bank].at[b]
        source = (xq, xk, xv, pr)[bank].at[b]
        off = 8 if bank == 3 else 16
        sums = [None] * TAPS
        for at, rows in spans:
            g = grad[at : at + rows, :]
            for j in range(TAPS):
                part = g * source[pl.ds(off + at - j, rows), :]
                part = jnp.sum(part.reshape(rows // 8, 8, LANE), axis=0)
                sums[j] = part if sums[j] is None else sums[j] + part
        for j in range(TAPS):
            acc[m, 4 * j + bank] = acc[m, 4 * j + bank] + sums[j]

    def interior(b, carry):
        m = lax.rem(b, tiles)
        lanes = lanes_of(b)
        for ref, i in ((xq, 0), (xk, 1), (xv, 2)):
            ref[b, 16 : 16 + length, :] = fb[i, :, lanes].astype(F32)
        xc[b, 0:length, :] = cb[:, lanes].astype(F32)
        q_rows(b, m, chunks(8, length))
        kv_rows(b, m, chunks(8, length))
        mixer_rows(b, m, chunks(16, length))
        product_rows(b, m, chunks(8, length - 8))
        filter_rows(b, m, 0, chunks(16, length))
        filter_rows(b, m, 1, chunks(8, length - 8))
        filter_rows(b, m, 2, chunks(8, length - 8))
        filter_rows(b, m, 3, chunks(16, length))
        return carry

    lax.fori_loop(0, blocks, interior, 0)
    for copy in halo[4:]:
        copy.start()
    hear(1)
    tell(2)
    for copy in halo[:4]:
        copy.wait_recv()

    def edge(ref, lanes, drop):
        return jnp.where(drop, 0.0, ref[:, lanes].astype(F32))

    def edges(b, carry):
        m = lax.rem(b, tiles)
        lanes = lanes_of(b)
        xq[b, 8:16, :] = edge(hl_q, lanes, first)
        xk[b, 0:16, :] = edge(hl_kv.at[0], lanes, first)
        xv[b, 0:16, :] = edge(hl_kv.at[1], lanes, first)
        xc[b, length : length + 8, :] = edge(hr_c, lanes, last)
        xq[b, 16 + length : 24 + length, :] = edge(hr_q, lanes, last)
        ends = [(0, 8), (length - 8, 8)]
        q_rows(b, m, [(0, 8), (length, 8)])
        kv_rows(b, m, [(-8, 16)])
        mixer_rows(b, m, [(0, 16)])
        product_rows(b, m, ends)
        filter_rows(b, m, 0, [(0, 16)])
        filter_rows(b, m, 1, ends)
        filter_rows(b, m, 2, ends)
        filter_rows(b, m, 3, [(0, 16)])
        return carry

    lax.fori_loop(0, blocks, edges, 0)
    out_mixed = pltpu.make_async_copy(mb, mixed_o, out_sem.at[0])
    out_mixed.start()

    lane_at = lax.broadcasted_iota(jnp.int32, (8, LANE), 1)
    for pair in range(4):
        parts = [
            jnp.sum(acc[m, 8 * pair : 8 * pair + 8], axis=1) for m in range(tiles)
        ]
        for g in range(n_f):
            m, off = divmod(g * portion, LANE)
            piece = pltpu.roll(parts[m], (LANE - off) % LANE, 1) if off else parts[m]
            if off + portion > LANE:
                rest = pltpu.roll(parts[m + 1], LANE - off, 1)
                piece = jnp.where(lane_at < LANE - off, piece, rest)
            for i in range(2):
                half, tap = divmod(2 * pair + i, 4)
                s1s[g * LO + half, tap] = piece[4 * i : 4 * i + 4]
    for d in range(1, nx):
        s = lax.rem(x8 + d, nx)
        copy = remote(s1s.at[s], s1r.at[x8], s1_ss.at[d], s1_rs.at[x8], row_dev(s))
        copy.start()
        kept.append(copy)
    s1r[x8] = s1s[x8]
    for d in range(1, nx):
        s = lax.rem(x8 + d, nx)
        remote(s1s.at[s], s1r.at[s], s1_ss.at[d], s1_rs.at[s], row_dev(s)).wait_recv()
    total = s1r[0]
    for s in range(1, nx):
        total = total + s1r[s]
    s2s[...] = total

    mine = lax.rem(y, 4)
    for d in far_first(ny):
        s = lax.rem(y + d, ny)
        copy = remote(
            s2s.at[lax.rem(s, 4)], s2r.at[y], s2_ss.at[d], s2_rs.at[y], dev(z, s, lo, f)
        )
        copy.start()
        kept.append(copy)
    s2r[y] = s2s[mine]
    for d in range(1, ny):
        s = lax.rem(y + d, ny)
        remote(
            s2s.at[mine], s2r.at[s], s2_ss.at[d], s2_rs.at[s], dev(z, s, lo, f)
        ).wait_recv()
    total = s2r[0]
    for s in range(1, ny):
        total = total + s2r[s]
    s3s[...] = total

    hear(2)
    for d in far_first(nz):
        s = lax.rem(z + d, nz)
        copy = remote(s3s, s3r.at[z], s3_ss.at[d], s3_rs.at[z], dev(s, y, lo, f))
        copy.start()
        kept.append(copy)
    s3r[z] = s3s[...]

    for copy in halo[4:]:
        copy.wait_recv()

    def second_pass(b, carry):
        m = lax.rem(b, tiles)
        lanes = lanes_of(b)
        xc[b, length + 8 : length + 16, :] = edge(lr_c, lanes, last)
        xq[b, 24 + length : 32 + length, :] = edge(lr_q, lanes, last)
        xk[b, 16 + length : 24 + length, :] = edge(lr_kv.at[0], lanes, last)
        xv[b, 16 + length : 24 + length, :] = edge(lr_kv.at[1], lanes, last)
        past = [(length, 8)]
        q_rows(b, m, [(length + 8, 8)])
        kv_rows(b, m, past)
        mixer_rows(b, m, past, keep=False)
        product_rows(b, m, past)
        for bank, grad in enumerate((gq.at[b], gk.at[b], gv.at[b])):
            w = taps(m, bank)
            for at, rows in chunks(0, length):
                gb[bank, at : at + rows, lanes] = fir(grad, at, rows, w, 1).astype(BF16)
        return carry

    lax.fori_loop(0, blocks, second_pass, 0)
    out_grads = pltpu.make_async_copy(gb, grads_o, out_sem.at[1])
    out_grads.start()

    for d in range(1, nz):
        s = lax.rem(z + d, nz)
        remote(s3s, s3r.at[s], s3_ss.at[d], s3_rs.at[s], dev(s, y, lo, f)).wait_recv()
    total = s3r[0]
    for s in range(1, nz):
        total = total + s3r[s]
    s4s[...] = total

    tap = lo * 4 + mine
    for i, (d, other) in enumerate(
        ((2, 1), (2, 0), (-1, 1), (1, 1), (-1, 0), (1, 0), (0, 1))
    ):
        device = dev(z, lax.rem(y + d + ny, ny), 1 - lo if other else lo, f)
        copy = remote(s4s, res.at[tap], s4_ss.at[i], s4_rs.at[tap], device)
        copy.start()
        kept.append(copy)
    out_res = pltpu.make_async_copy(s4s, res.at[tap], out_sem.at[2])
    out_res.start()
    for d in range(1, LO * 4):
        s = lax.rem(tap + d, LO * 4)
        remote(s4s, res.at[s], s4_ss.at[0], s4_rs.at[s], nxt).wait_recv()

    for copy in kept:
        copy.wait_send()
    out_mixed.wait()
    out_grads.wait()
    out_res.wait()


def write(factor, mixed, grads, res, mixed_o, grads_o, filt_o, big, small, done, sem):
    pieces = [(res, small)] + [(mixed, big.at[3])]
    pieces += [(grads.at[i], big.at[i]) for i in range(3)]
    reads = [
        pltpu.make_async_copy(src, dst, sem.at[0, i])
        for i, (src, dst) in enumerate(pieces)
    ]
    for copy in reads:
        copy.start()
    reads[0].wait()
    portion = filt_o.shape[2]
    for j in range(TAPS):
        done[j] = small[j][:, :portion] * factor
    outs = [(done, filt_o), (big.at[3], mixed_o)]
    outs += [(big.at[i], grads_o.at[i]) for i in range(3)]
    writes = [
        pltpu.make_async_copy(src, dst, sem.at[1, i])
        for i, (src, dst) in enumerate(outs)
    ]
    writes[0].start()
    for i in range(1, 5):
        reads[i].wait()
        writes[i].start()
    for copy in writes:
        copy.wait()


def per_device(n_ctx, n_f, ny, features, cotangent, master_filters):
    _, length, width = features.shape
    portion = master_filters.shape[2]
    groups = portion * n_f
    repeats = width // groups
    count_all = length * n_ctx * repeats * n_f
    factor = 1.0 / math.sqrt(count_all)
    nz = n_ctx // (LO * ny)
    nx = n_f * LO
    blocks = width // LANE
    tiles = groups // LANE
    vm = pltpu.VMEM
    dma = pltpu.SemaphoreType.DMA
    scratch = [
        vm((3, length, width), BF16), vm((length, width), BF16),
        vm((length, width), BF16), vm((3, length, width), BF16),
        vm((8, width), BF16), vm((2, 16, width), BF16),
        vm((8, width), BF16), vm((8, width), BF16),
        vm((8, width), BF16), vm((8, width), BF16), vm((2, 8, width), BF16),
        vm((n_f, TAPS, 4, portion), F32), vm((tiles, TAPS, 4, LANE), F32),
    ]
    scratch += [vm((blocks, length + 32, LANE), F32)] * 3
    scratch += [vm((blocks, length + 16, LANE), F32)] * 6
    scratch += [vm((blocks, length + 8, LANE), F32)] * 3
    scratch += [
        vm((tiles, 32, 8, LANE), F32),
        vm((nx, 4, 4, LANE), F32), vm((nx, 4, 4, LANE), F32),
        vm((4, 4, LANE), F32), vm((ny, 4, LANE), F32),
        vm((4, LANE), F32), vm((nz, 4, LANE), F32), vm((4, LANE), F32),
        dma((3,)), dma((7,)), dma((7,)), dma((n_f,)), dma((n_f,)),
        dma((nx,)), dma((nx,)), dma((ny,)), dma((ny,)), dma((nz,)), dma((nz,)),
        dma((7,)), dma((8,)), dma((3,)), pltpu.SemaphoreType.REGULAR((3, 2)),
    ]
    anywhere = pl.BlockSpec(memory_space=pl.ANY)
    big = (
        jax.ShapeDtypeStruct((length, width), BF16),
        jax.ShapeDtypeStruct((3, length, width), BF16),
    )
    mixed, grads, res = pl.pallas_call(
        functools.partial(kernel, n_ctx, n_f, ny),
        out_shape=big + (jax.ShapeDtypeStruct((8, 4, LANE), F32),),
        in_specs=[anywhere] * 3,
        out_specs=(anywhere,) * 3,
        scratch_shapes=scratch,
        compiler_params=pltpu.CompilerParams(
            collective_id=0, has_side_effects=True, vmem_limit_bytes=ALL_VMEM
        ),
    )(features, cotangent, jnp.transpose(master_filters, (1, 0, 2)))
    mixed, grads, filters = pl.pallas_call(
        functools.partial(write, factor),
        out_shape=big + (jax.ShapeDtypeStruct((TAPS, 4, portion), F32),),
        in_specs=[anywhere] * 3,
        out_specs=(anywhere,) * 3,
        scratch_shapes=[
            vm((4, length, width), BF16), vm((8, 4, LANE), F32),
            vm((TAPS, 4, portion), F32), dma((2, 5)),
        ],
        compiler_params=pltpu.CompilerParams(vmem_limit_bytes=ALL_VMEM),
    )(mixed, grads, res)
    return mixed, grads, jnp.transpose(filters, (1, 0, 2))


def solution(mesh, ny=NY):
    return jax.shard_map(
        functools.partial(per_device, mesh.shape["ctx"], mesh.shape["fsdp"], ny),
        mesh=mesh,
        in_specs=(P(None, "ctx", "fsdp"), P("ctx", "fsdp"), P(None, None, "fsdp")),
        out_specs=(P("ctx", "fsdp"), P(None, "ctx", "fsdp"), P(None, None, "fsdp")),
        check_vma=False,
    )
```

time: 61.2 us -> 52.3 us (0.85)
  the two profiles are of different devices: /device:TPU:2 before, /device:TPU:1 now
where the time goes in v2:
time: 52.3 us; the launch traced here: 51.6 us
  Pallas kernels  51 us (98%)
  between operations  0.64 us (1%)
    pallas_call x1, Pallas kernels, per_device(): pl.pallas_call(functools.partial(kernel, n_ctx, n_f, ny), out_shape=big +...  48.8 us
    pallas_call x1, Pallas kernels, per_device(): pl.pallas_call(functools.partial(write, factor), out_shape=big + (jax.Sha...  2.23 us

profile of v2, /device:TPU:1, one launch (start us, length us, event | category | flops | bytes accessed | tf_op | source)
XLA Modules:
  0.0 51.6 jit_solution(9965289920680093391)
XLA Ops:
  0.6 48.8 %shard_map.58 = (bf16[128,1536]{1,0:T(8,128)(2,1)}, bf16[3,128,1536]{2,1,0:T(8,128)(2,1)}, f32[8,4,128]{2,1,0:T(4,128)}) custom-call(bf16[3,128,1536]{2,1,0:T(8,128)(2,1)} %feat.1, bf16[128,1536]{1,0:T(8,128)(2,1)} %cot.1, f32[7,4,96]{2,1,0:T(4,128)} %bitcast.2), custom_call_target="tpu_custom_call" | custom-call | tf_op jit(solution)/shard_map/pallas_call | solution.py:437
  49.4 2.2 %shard_map.59 = (bf16[128,1536]{1,0:T(8,128)(2,1)}, bf16[3,128,1536]{2,1,0:T(8,128)(2,1)}, f32[7,4,96]{2,1,0:T(4,128)}) custom-call(bf16[128,1536]{1,0:T(8,128)(2,1)} %get-tuple-element.9.mixed, bf16[3,128,1536]{2,1,0:T(8,128)(2,1)} %get-tuple-element.10.grads, f32[8,4,128]{2,1,0:T(4,128)} %get-tuple-element.11.res), custom_call_target="tpu_custom_call" | custom-call | tf_op jit(solution)/shard_map/pallas_call | solution.py:447

commit v3 on v2

--- a/solution.py
+++ b/solution.py
@@ -111,11 +111,10 @@
     tell(0)
 
     kept = []
-    for d in range(1, n_f):
-        copy = remote(
-            mast, wg.at[f], filt_ss.at[d], filt_rs.at[f],
-            (ctx, lax.rem(f + d, n_f)),
-        )
+    beside = f + 1 - 2 * lax.rem(f, 2)
+    across = lax.rem(f + 2, n_f)
+    for d, target in ((1, beside), (2, across), (3, lax.rem(beside + 2, n_f))):
+        copy = remote(mast, wg.at[f], filt_ss.at[d], filt_rs.at[f], (ctx, target))
         copy.start()
         kept.append(copy)
     halo_plan = [
@@ -137,16 +136,30 @@
 
     for copy in loads:
         copy.wait()
-    for d in range(1, n_f):
-        src = lax.rem(f + d, n_f)
-        remote(mast, wg.at[src], filt_ss.at[d], filt_rs.at[src], (ctx, src)).wait_recv()
-    hear(0)
-    tell(1)
-    for j in range(TAPS):
-        whole = jnp.concatenate([wg[i, j] for i in range(n_f)], axis=1)
-        whole = whole.astype(BF16).astype(F32)
-        for m in range(tiles):
-            wv[m, j] = whole[:, m * LANE : (m + 1) * LANE]
+    def hear_filters(src, i):
+        remote(mast, wg.at[src], filt_ss.at[i], filt_rs.at[src], (ctx, src)).wait_recv()
+
+    def place(tile, held):
+        at = tile * LANE
+        for j in range(TAPS):
+            parts = []
+            for i in held:
+                low, high = max(at, i * portion), min(at + LANE, (i + 1) * portion)
+                if low < high:
+                    parts.append(wg[i, j, :, low - i * portion : high - i * portion])
+            whole = jnp.concatenate(parts, axis=1)
+            wv[tile, j] = whole.astype(BF16).astype(F32)
+
+    pair = lax.div(f, 2)
+    hear_filters(beside, 1)
+
+    @pl.when(pair == 0)
+    def _():
+        place(0, (0, 1))
+
+    @pl.when(pair == 1)
+    def _():
+        place(2, (2, 3))
 
     def taps(m, bank):
         return [wv[m, j, pl.ds(bank, 1), :] for j in range(TAPS)]
@@ -226,7 +239,32 @@
         filter_rows(b, m, 3, chunks(16, length))
         return carry
 
-    lax.fori_loop(0, blocks, interior, 0)
+    own = 2 * pair
+
+    def own_tile(i, carry):
+        return interior(own + tiles * i, carry)
+
+    def other_tiles(i, carry):
+        m = jnp.where(lax.rem(i, 2) == 0, 1, 2 - own)
+        return interior(m + tiles * lax.div(i, 2), carry)
+
+    lax.fori_loop(0, blocks // tiles, own_tile, 0)
+    for i in range(2):
+        hear_filters(2 - own + i, 2 + i)
+    hear(0)
+    tell(1)
+
+    @pl.when(pair == 0)
+    def _():
+        place(1, range(n_f))
+        place(2, range(n_f))
+
+    @pl.when(pair == 1)
+    def _():
+        place(0, range(n_f))
+        place(1, range(n_f))
+
+    lax.fori_loop(0, blocks - blocks // tiles, other_tiles, 0)
     for copy in halo[4:]:
         copy.start()
     hear(1)

time: 52.3 us -> 51.4 us (0.983)
  the two profiles are of different devices: /device:TPU:1 before, /device:TPU:8 now
where the time goes in v3:
time: 51.4 us; the launch traced here: 51.1 us
  Pallas kernels  50.5 us (98%)
  between operations  0.64 us (1%)
    pallas_call x1, Pallas kernels, per_device(): pl.pallas_call(functools.partial(kernel, n_ctx, n_f, ny), out_shape=big +...  48.3 us
    pallas_call x1, Pallas kernels, per_device(): pl.pallas_call(functools.partial(write, factor), out_shape=big + (jax.Sha...  2.23 us

profile of v3, /device:TPU:8, one launch (start us, length us, event | category | flops | bytes accessed | tf_op | source)
XLA Modules:
  0.0 51.1 jit_solution(10020082541491158743)
XLA Ops:
  0.6 48.3 %shard_map.58 = (bf16[128,1536]{1,0:T(8,128)(2,1)}, bf16[3,128,1536]{2,1,0:T(8,128)(2,1)}, f32[8,4,128]{2,1,0:T(4,128)}) custom-call(bf16[3,128,1536]{2,1,0:T(8,128)(2,1)} %feat.1, bf16[128,1536]{1,0:T(8,128)(2,1)} %cot.1, f32[7,4,96]{2,1,0:T(4,128)} %bitcast.2), custom_call_target="tpu_custom_call" | custom-call | tf_op jit(solution)/shard_map/pallas_call | solution.py:475
  48.9 2.2 %shard_map.59 = (bf16[128,1536]{1,0:T(8,128)(2,1)}, bf16[3,128,1536]{2,1,0:T(8,128)(2,1)}, f32[7,4,96]{2,1,0:T(4,128)}) custom-call(bf16[128,1536]{1,0:T(8,128)(2,1)} %get-tuple-element.9.mixed, bf16[3,128,1536]{2,1,0:T(8,128)(2,1)} %get-tuple-element.10.grads, f32[8,4,128]{2,1,0:T(4,128)} %get-tuple-element.11.res), custom_call_target="tpu_custom_call" | custom-call | tf_op jit(solution)/shard_map/pallas_call | solution.py:485

commit v4 on v3

--- a/solution.py
+++ b/solution.py
@@ -31,9 +31,9 @@
     mixed_o, grads_o, res,
     fb, cb, mb, gb, hl_q, hl_kv, hr_c, hr_q, lr_c, lr_q, lr_kv, wg, wv,
     xq, xk, xv, xc, qc, kc, vc, pr, gm, gq, gk, gv, acc,
-    s1s, s1r, s2s, s2r, s3s, s3r, s4s,
+    s1s, s1r, s3s, s3r, s4s,
     load_sem, halo_ss, halo_rs, filt_ss, filt_rs,
-    s1_ss, s1_rs, s2_ss, s2_rs, s3_ss, s3_rs, s4_ss, s4_rs, out_sem, near_sem,
+    s1_ss, s1_rs, s3_ss, s3_rs, s4_ss, s4_rs, out_sem, near_sem,
 ):
     length = fb.shape[1]
     blocks = fb.shape[2] // LANE
@@ -75,7 +75,7 @@
     if nz > 1:
         partners += [at_z(1), at_z(-1)]
     if ny > 1:
-        partners += [at_y(1), at_y(-1)]
+        partners += [at_y(1), at_y(-1), at_y(2), at_y(-2)]
     partners += [row_dev(lax.rem(x8 + d, nx)) for d in range(1, nx)]
     barrier = pltpu.get_barrier_semaphore()
     for device in partners:
@@ -92,21 +92,23 @@
     acc[...] = jnp.zeros_like(acc)
     pl.semaphore_wait(barrier, len(partners))
 
+    steps_z = [r for r in (1, 2, 4) if r < nz // 2]
+    signals = [
+        [at_z(d) for r in steps_z[i : i + 1] for d in (r, -r)] for i in range(3)
+    ]
+    signals[0] += [at_y(d) for d in (1, -1, 2, -2)]
+    signals[1] += [at_y(d) for d in (2, -2)]
+
     def tell(step):
-        reach = 1 << step
-        for i, (n, at) in enumerate(((nz, at_z), (ny, at_y))):
-            if reach < n // 2:
-                for d in (reach, -reach):
-                    pl.semaphore_signal(
-                        near_sem.at[step, i], inc=1, device_id=at(d),
-                        device_id_type=pl.DeviceIdType.MESH,
-                    )
+        for device in signals[step]:
+            pl.semaphore_signal(
+                near_sem.at[step], inc=1, device_id=device,
+                device_id_type=pl.DeviceIdType.MESH,
+            )
 
     def hear(step):
-        reach = 1 << step
-        for i, n in enumerate((nz, ny)):
-            if reach < n // 2:
-                pl.semaphore_wait(near_sem.at[step, i], 2)
+        if signals[step]:
+            pl.semaphore_wait(near_sem.at[step], len(signals[step]))
 
     tell(0)
 
@@ -312,42 +314,27 @@
             for i in range(2):
                 half, tap = divmod(2 * pair + i, 4)
                 s1s[g * LO + half, tap] = piece[4 * i : 4 * i + 4]
-    for d in range(1, nx):
-        s = lax.rem(x8 + d, nx)
-        copy = remote(s1s.at[s], s1r.at[x8], s1_ss.at[d], s1_rs.at[x8], row_dev(s))
-        copy.start()
-        kept.append(copy)
-    s1r[x8] = s1s[x8]
-    for d in range(1, nx):
-        s = lax.rem(x8 + d, nx)
-        remote(s1s.at[s], s1r.at[s], s1_ss.at[d], s1_rs.at[s], row_dev(s)).wait_recv()
-    total = s1r[0]
-    for s in range(1, nx):
-        total = total + s1r[s]
-    s2s[...] = total
-
     mine = lax.rem(y, 4)
-    for d in far_first(ny):
-        s = lax.rem(y + d, ny)
-        copy = remote(
-            s2s.at[lax.rem(s, 4)], s2r.at[y], s2_ss.at[d], s2_rs.at[y], dev(z, s, lo, f)
-        )
-        copy.start()
-        kept.append(copy)
-    s2r[y] = s2s[mine]
-    for d in range(1, ny):
-        s = lax.rem(y + d, ny)
-        remote(
-            s2s.at[mine], s2r.at[s], s2_ss.at[d], s2_rs.at[s], dev(z, s, lo, f)
-        ).wait_recv()
-    total = s2r[0]
-    for s in range(1, ny):
-        total = total + s2r[s]
-    s3s[...] = total
+    for d in far_first(ny) + [0]:
+        y_ = lax.rem(y + d, ny)
+        for e in range(nx) if d else range(1, nx):
+            s = lax.rem(x8 + e, nx)
+            remote(
+                s1s.at[s, lax.rem(y_, 4)], s1r.at[y * nx + x8], s1_ss.at[0], s1_rs.at[0],
+                dev(z, y_, lax.rem(s, LO), lax.div(s, LO)),
+            ).start()
+    s1r[y * nx + x8] = s1s[x8, mine]
+    others = s1r.at[pl.ds(0, ny * nx - 1)]
+    every = remote(others, others, s1_ss.at[0], s1_rs.at[0], nxt)
+    every.wait_recv()
+    sums = [s1r[i] for i in range(ny * nx)]
+    while len(sums) > 1:
+        sums = [a + b for a, b in zip(sums[::2], sums[1::2], strict=True)]
+    s3s[...] = sums[0]
 
     hear(2)
-    for d in far_first(nz):
-        s = lax.rem(z + d, nz)
+    for d in range(1, nz):
+        s = jnp.where(d <= z, d - 1, d)
         copy = remote(s3s, s3r.at[z], s3_ss.at[d], s3_rs.at[z], dev(s, y, lo, f))
         copy.start()
         kept.append(copy)
@@ -402,6 +389,7 @@
 
     for copy in kept:
         copy.wait_send()
+    every.wait_send()
     out_mixed.wait()
     out_grads.wait()
     out_res.wait()
@@ -460,12 +448,11 @@
     scratch += [vm((blocks, length + 8, LANE), F32)] * 3
     scratch += [
         vm((tiles, 32, 8, LANE), F32),
-        vm((nx, 4, 4, LANE), F32), vm((nx, 4, 4, LANE), F32),
-        vm((4, 4, LANE), F32), vm((ny, 4, LANE), F32),
+        vm((nx, 4, 4, LANE), F32), vm((ny * nx, 4, LANE), F32),
         vm((4, LANE), F32), vm((nz, 4, LANE), F32), vm((4, LANE), F32),
         dma((3,)), dma((7,)), dma((7,)), dma((n_f,)), dma((n_f,)),
-        dma((nx,)), dma((nx,)), dma((ny,)), dma((ny,)), dma((nz,)), dma((nz,)),
-        dma((7,)), dma((8,)), dma((3,)), pltpu.SemaphoreType.REGULAR((3, 2)),
+        dma((1,)), dma((1,)), dma((nz,)), dma((nz,)),
+        dma((7,)), dma((8,)), dma((3,)), pltpu.SemaphoreType.REGULAR((3,)),
     ]
     anywhere = pl.BlockSpec(memory_space=pl.ANY)
     big = (

time: 51.4 us -> 49.5 us (0.963)
  the two profiles are of different devices: /device:TPU:8 before, /device:TPU:1 now
where the time goes in v4:
time: 49.5 us; the launch traced here: 49.1 us
  Pallas kernels  48.5 us (98%)
  between operations  0.64 us (1%)
    pallas_call x1, Pallas kernels, per_device(): pl.pallas_call(functools.partial(kernel, n_ctx, n_f, ny), out_shape=big +...  46.3 us
    pallas_call x1, Pallas kernels, per_device(): pl.pallas_call(functools.partial(write, factor), out_shape=big + (jax.Sha...  2.23 us

profile of v4, /device:TPU:1, one launch (start us, length us, event | category | flops | bytes accessed | tf_op | source)
XLA Modules:
  0.0 49.1 jit_solution(12574594362228560696)
XLA Ops:
  0.6 46.3 %shard_map.58 = (bf16[128,1536]{1,0:T(8,128)(2,1)}, bf16[3,128,1536]{2,1,0:T(8,128)(2,1)}, f32[8,4,128]{2,1,0:T(4,128)}) custom-call(bf16[3,128,1536]{2,1,0:T(8,128)(2,1)} %feat.1, bf16[128,1536]{1,0:T(8,128)(2,1)} %cot.1, f32[7,4,96]{2,1,0:T(4,128)} %bitcast.2), custom_call_target="tpu_custom_call" | custom-call | tf_op jit(solution)/shard_map/pallas_call | solution.py:462
  46.9 2.2 %shard_map.59 = (bf16[128,1536]{1,0:T(8,128)(2,1)}, bf16[3,128,1536]{2,1,0:T(8,128)(2,1)}, f32[7,4,96]{2,1,0:T(4,128)}) custom-call(bf16[128,1536]{1,0:T(8,128)(2,1)} %get-tuple-element.9.mixed, bf16[3,128,1536]{2,1,0:T(8,128)(2,1)} %get-tuple-element.10.grads, f32[8,4,128]{2,1,0:T(4,128)} %get-tuple-element.11.res), custom_call_target="tpu_custom_call" | custom-call | tf_op jit(solution)/shard_map/pallas_call | solution.py:472
